TPU v7x, 32 devices: a whole 2x2x4 slice. The times are simulated.
32 devices in a mesh: dp: 8 (over z, y), expert: 4 (over x, core).
Axes of the slice: x: 2, y: 2, z: 4, core: 2. Of those that a mesh axis runs over, the one named last changes fastest.
Arguments:
- hidden_in: float32 [4, 2560, 1536], P('expert', 'dp'), may hold values from -6 to 6
- gain_attn: float32 [1536], replicated, may hold values from 0.5 to 1.5
- w_query: bfloat16 [1536, 1536], replicated, may hold values from -0.15625 to 0.15625
- w_key: bfloat16 [1536, 512], replicated, may hold values from -0.15625 to 0.15625
- w_value: bfloat16 [1536, 512], replicated, may hold values from -0.15625 to 0.15625
- w_output: bfloat16 [1536, 1536], replicated, may hold values from -1.25 to 1.25
- gain_mlp: float32 [1536], replicated, may hold values from 0.5 to 1.5
- w_router: bfloat16 [1536, 40], replicated, may hold values from -0.078125 to 0.078125
- w_gate: bfloat16 [40, 1536, 512], P('expert'), may hold values from -0.15625 to 0.15625
- w_up: bfloat16 [40, 1536, 512], P('expert'), may hold values from -0.15625 to 0.15625
- w_down: bfloat16 [40, 512, 1536], P('expert'), may hold values from -1 to 1
- expert_ids: int32 [4, 2560, 8], P('expert', 'dp'), may hold values from 0 to 39, all different within a row
- slot_order: int32 [4, 8, 2560], P('expert', 'dp'), may hold values from 0 to 2559, each once within a row
- grad_out: float32 [4, 2560, 1536], P('expert', 'dp'), may hold values from -6 to 6
Outputs:
- hidden_out: float32 [4, 2560, 1536], P('expert', 'dp')
- grad_in: float32 [4, 2560, 1536], P('expert', 'dp')
- grad_gain_attn: float32 [1536], P(('dp', 'expert'))
- grad_query: float32 [1536, 1536], P(('dp', 'expert'))
- grad_key: float32 [1536, 512], P(('dp', 'expert'))
- grad_value: float32 [1536, 512], P(('dp', 'expert'))
- grad_output: float32 [1536, 1536], P(('dp', 'expert'))
- grad_gain_mlp: float32 [1536], P(('dp', 'expert'))
- grad_router: float32 [1536, 40], P(('dp', 'expert'))
- grad_gate: float32 [40, 1536, 512], P('expert', 'dp')
- grad_up: float32 [40, 1536, 512], P('expert', 'dp')
- grad_down: float32 [40, 512, 1536], P('expert', 'dp')
Inputs may be any that keep to these rules, and one draw needn't show every extreme that they name: `expert_ids`: each token names 8 different experts. `slot_order`: for every sequence and block, the 2560 ranks of the block's pairs are each of 0 to 2559 once.
All inputs are finite; a program needn't handle non-finite values.
Results may differ from a plain program's by a relative error of at most 0.019.
Values may be sent and summed in bfloat16 or wider, within the bound.
A program may use at most 320 MiB of HBM per device.

v0:
```python
import math
import jax
import jax.numpy as jnp
from jax import lax
from jax.sharding import PartitionSpec as P

HEADS = 24
KV_HEADS = 8
HEAD_DIM = 64
EPS = 1e-05
MASKED = -1e30


def rotary_tables(positions):
    half = HEAD_DIM // 2
    frequency = jnp.exp(-math.log(10000.0) * jnp.arange(half, dtype=jnp.float32) * 2.0 / HEAD_DIM)
    angles = positions.astype(jnp.float32)[:, None] * frequency[None, :]
    return (jnp.cos(angles)[:, None, :], jnp.sin(angles)[:, None, :])


def rotate(values, cosine, sine):
    half = values.shape[-1] // 2
    first = values[..., :half]
    second = values[..., half:]
    return jnp.concatenate(
        [first * cosine - second * sine, second * cosine + first * sine], axis=-1
    )


def rotate_back(values, cosine, sine):
    half = values.shape[-1] // 2
    first = values[..., :half]
    second = values[..., half:]
    return jnp.concatenate(
        [first * cosine + second * sine, second * cosine - first * sine], axis=-1
    )


def assign_slots(row_chosen, row_ranks, all_experts, capacity):
    pairs = row_chosen.shape[0]
    by_rank = jnp.zeros((pairs,), jnp.int32).at[row_ranks].set(jnp.arange(pairs, dtype=jnp.int32))
    ordered = row_chosen[by_rank]
    table = (ordered[:, None] == jnp.arange(all_experts, dtype=jnp.int32)[None, :]).astype(
        jnp.int32
    )
    before = jnp.sum(table * (jnp.cumsum(table, axis=0) - 1), axis=1)
    slot = before[row_ranks]
    target = jnp.where(slot < capacity, row_chosen * capacity + slot, all_experts * capacity)
    owner = (
        jnp.full((all_experts * capacity,), pairs, jnp.int32)
        .at[target]
        .set(jnp.arange(pairs, dtype=jnp.int32), mode="drop")
    )
    return (target, owner)


def body(
    hidden_in,
    gain_attn,
    w_query,
    w_key,
    w_value,
    w_output,
    gain_mlp,
    w_router,
    w_gate,
    w_up,
    w_down,
    expert_ids,
    slot_order,
    grad_out,
):
    inputs = hidden_in[0]
    cotangent = grad_out[0]
    chosen = expert_ids[0]
    tokens, width = inputs.shape
    top = chosen.shape[1]
    local_experts = w_gate.shape[0]
    peers = lax.axis_size("expert")
    all_experts = local_experts * peers
    pairs = tokens * top
    capacity = pairs // all_experts
    shards = lax.axis_size("dp")
    index = lax.axis_index("dp")
    length = shards * tokens
    block = math.gcd(length, 512)
    groups = HEADS // KV_HEADS
    scale = HEAD_DIM ** (-0.5)
    query_pos = index * tokens + jnp.arange(tokens, dtype=jnp.int32)
    cosine, sine = rotary_tables(query_pos)
    count = ((index + 1) * tokens + block - 1) // block
    inv_one = lax.rsqrt(jnp.mean(inputs * inputs, axis=-1, keepdims=True) + EPS)
    normed = (inputs * inv_one * gain_attn).astype(jnp.bfloat16)
    query_pre = jnp.dot(normed, w_query, preferred_element_type=jnp.float32).reshape(
        tokens, HEADS, HEAD_DIM
    )
    queries = rotate(query_pre, cosine, sine).astype(jnp.bfloat16)
    key_pre = jnp.dot(normed, w_key, preferred_element_type=jnp.float32).reshape(
        tokens, KV_HEADS, HEAD_DIM
    )
    keys_low = rotate(key_pre, cosine, sine).astype(jnp.bfloat16)
    values_low = (
        jnp.dot(normed, w_value, preferred_element_type=jnp.float32)
        .astype(jnp.bfloat16)
        .reshape(tokens, KV_HEADS, HEAD_DIM)
    )
    keys_all, values_all = (
        lax.all_gather(keys_low, "dp", axis=0, tiled=True),
        lax.all_gather(values_low, "dp", axis=0, tiled=True),
    )
    query_groups = queries.reshape(tokens, KV_HEADS, groups, HEAD_DIM)

    def block_scores(key_block, start):
        raw = (
            jnp.einsum(
                "qkgd,skd->kgqs", query_groups, key_block, preferred_element_type=jnp.float32
            )
            * scale
        )
        key_pos = start + jnp.arange(block, dtype=jnp.int32)
        allowed = key_pos[None, :] <= query_pos[:, None]
        return jnp.where(allowed, raw, MASKED)

    def stats_step(step, carry):
        running, total = carry
        scores = block_scores(
            lax.dynamic_slice_in_dim(keys_all, step * block, block, 0), step * block
        )
        newest = jnp.maximum(running, jnp.max(scores, axis=-1))
        total = total * jnp.exp(running - newest) + jnp.sum(
            jnp.exp(scores - newest[..., None]), axis=-1
        )
        return (newest, total)

    stat_init = (
        jnp.full((KV_HEADS, groups, tokens), MASKED, jnp.float32),
        jnp.zeros((KV_HEADS, groups, tokens), jnp.float32),
    )
    running, total = lax.fori_loop(0, count, stats_step, stat_init)
    log_total = running + jnp.log(total)

    def output_step(step, accum):
        start = step * block
        scores = block_scores(lax.dynamic_slice_in_dim(keys_all, start, block, 0), start)
        probs = jnp.exp(scores - log_total[..., None]).astype(jnp.bfloat16)
        value_block = lax.dynamic_slice_in_dim(values_all, start, block, 0)
        return accum + jnp.einsum(
            "kgqs,skd->qkgd", probs, value_block, preferred_element_type=jnp.float32
        )

    attended_groups = lax.fori_loop(
        0, count, output_step, jnp.zeros((tokens, KV_HEADS, groups, HEAD_DIM), jnp.float32)
    )
    attended = attended_groups.reshape(tokens, HEADS * HEAD_DIM)
    attended_low = attended.astype(jnp.bfloat16)
    branch = jnp.dot(attended_low, w_output, preferred_element_type=jnp.float32)
    middle = inputs + branch
    inv_two = lax.rsqrt(jnp.mean(middle * middle, axis=-1, keepdims=True) + EPS)
    normed_two = (middle * inv_two * gain_mlp).astype(jnp.bfloat16)
    logits = jnp.dot(normed_two, w_router, preferred_element_type=jnp.float32)
    onehot = (chosen[:, :, None] == jnp.arange(all_experts, dtype=jnp.int32)[None, None, :]).astype(
        jnp.float32
    )
    picked = jnp.sum(onehot * logits[:, None, :], axis=-1)
    gates = jax.nn.softmax(picked, axis=-1)
    target, owner = assign_slots(chosen.reshape(pairs), slot_order[0, 0], all_experts, capacity)
    valid = owner < pairs
    source = jnp.minimum(owner, pairs - 1)
    rows_send = jnp.where(valid[:, None], normed_two[source // top], 0).reshape(
        peers, local_experts, capacity, width
    )
    received = lax.all_to_all(rows_send, "expert", split_axis=0, concat_axis=0, tiled=True)
    gate_pre = jnp.einsum("necd,edf->necf", received, w_gate, preferred_element_type=jnp.float32)
    up_pre = jnp.einsum("necd,edf->necf", received, w_up, preferred_element_type=jnp.float32)
    hidden = (jax.nn.silu(gate_pre) * up_pre).astype(jnp.bfloat16)
    result = jnp.einsum(
        "necf,efd->necd", hidden, w_down, preferred_element_type=jnp.float32
    ).astype(jnp.bfloat16)
    returned = lax.all_to_all(result, "expert", split_axis=0, concat_axis=0, tiled=True)
    returned, received, gate_pre, up_pre = (returned, received, gate_pre, up_pre)
    zero_row = jnp.zeros((1, width), jnp.bfloat16)
    pair_out = jnp.concatenate([returned.reshape(all_experts * capacity, width), zero_row], axis=0)[
        target
    ].reshape(tokens, top, width)
    mixed = jnp.einsum("tk,tkd->td", gates, pair_out, preferred_element_type=jnp.float32)
    hidden_out = middle + mixed
    dy_pairs = (
        (gates[:, :, None] * cotangent[:, None, :]).astype(jnp.bfloat16).reshape(pairs, width)
    )
    dy_send = jnp.where(valid[:, None], dy_pairs[source], 0).reshape(
        peers, local_experts, capacity, width
    )
    dy_received = lax.all_to_all(dy_send, "expert", split_axis=0, concat_axis=0, tiled=True)
    sigmoid_gate = jax.nn.sigmoid(gate_pre)
    silu_gate = gate_pre * sigmoid_gate
    hidden = (silu_gate * up_pre).astype(jnp.bfloat16)
    grad_down_part = jnp.einsum(
        "necf,necd->efd", hidden, dy_received, preferred_element_type=jnp.float32
    )
    d_hidden = jnp.einsum("necd,efd->necf", dy_received, w_down, preferred_element_type=jnp.float32)
    d_gate = (d_hidden * up_pre * sigmoid_gate * (1.0 + gate_pre * (1.0 - sigmoid_gate))).astype(
        jnp.bfloat16
    )
    d_up = (d_hidden * silu_gate).astype(jnp.bfloat16)
    grad_gate_part = jnp.einsum(
        "necd,necf->edf", received, d_gate, preferred_element_type=jnp.float32
    )
    grad_up_part = jnp.einsum("necd,necf->edf", received, d_up, preferred_element_type=jnp.float32)
    gate_total, up_total, down_total = (
        lax.psum_scatter(
            grad_gate_part.astype(jnp.bfloat16), "dp", scatter_dimension=1, tiled=True
        ).astype(jnp.float32),
        lax.psum_scatter(
            grad_up_part.astype(jnp.bfloat16), "dp", scatter_dimension=1, tiled=True
        ).astype(jnp.float32),
        lax.psum_scatter(
            grad_down_part.astype(jnp.bfloat16), "dp", scatter_dimension=1, tiled=True
        ).astype(jnp.float32),
    )
    d_rows = jnp.einsum("necf,edf->necd", d_gate, w_gate, preferred_element_type=jnp.float32)
    d_rows = (
        d_rows + jnp.einsum("necf,edf->necd", d_up, w_up, preferred_element_type=jnp.float32)
    ).astype(jnp.bfloat16)
    d_back = lax.all_to_all(d_rows, "expert", split_axis=0, concat_axis=0, tiled=True)
    d_pairs = jnp.concatenate([d_back.reshape(all_experts * capacity, width), zero_row], axis=0)[
        target
    ].reshape(tokens, top, width)
    d_normed_two = jnp.sum(d_pairs, axis=1, dtype=jnp.float32)
    d_gates = jnp.einsum("td,tkd->tk", cotangent, pair_out, preferred_element_type=jnp.float32)
    d_picked = gates * (d_gates - jnp.sum(gates * d_gates, axis=-1, keepdims=True))
    d_logits = jnp.sum(onehot * d_picked[:, :, None], axis=1).astype(jnp.bfloat16)
    grad_router_part = jnp.einsum(
        "td,te->de", normed_two, d_logits, preferred_element_type=jnp.float32
    )
    d_normed_two = d_normed_two + jnp.einsum(
        "te,de->td", d_logits, w_router, preferred_element_type=jnp.float32
    )
    scaled_two = d_normed_two * gain_mlp
    grad_gain_mlp_part = jnp.sum(d_normed_two * middle * inv_two, axis=0)
    d_middle = (
        cotangent
        + inv_two * scaled_two
        - middle * inv_two**3 * jnp.mean(middle * scaled_two, axis=-1, keepdims=True)
    )
    d_branch = d_middle.astype(jnp.bfloat16)
    grad_output_part = jnp.einsum(
        "tf,td->fd", attended_low, d_branch, preferred_element_type=jnp.float32
    )
    d_attended = jnp.einsum(
        "td,fd->tf", d_branch, w_output, preferred_element_type=jnp.float32
    ).astype(jnp.bfloat16)
    d_groups = d_attended.reshape(tokens, KV_HEADS, groups, HEAD_DIM)
    delta = jnp.einsum(
        "qkgd,qkgd->kgq", d_groups, attended_groups, preferred_element_type=jnp.float32
    )
    keys_back, values_back = (
        lax.all_gather(keys_low, "dp", axis=0, tiled=True),
        lax.all_gather(values_low, "dp", axis=0, tiled=True),
    )

    def grad_step(step, carry):
        d_query, d_keys, d_values = carry
        start = step * block
        key_block = lax.dynamic_slice_in_dim(keys_back, start, block, 0)
        value_block = lax.dynamic_slice_in_dim(values_back, start, block, 0)
        scores = block_scores(key_block, start)
        probs = jnp.exp(scores - log_total[..., None])
        probs_low = probs.astype(jnp.bfloat16)
        d_probs = jnp.einsum(
            "qkgd,skd->kgqs", d_groups, value_block, preferred_element_type=jnp.float32
        )
        d_scores = (probs * (d_probs - delta[..., None])).astype(jnp.bfloat16)
        d_query = d_query + jnp.einsum(
            "kgqs,skd->qkgd", d_scores, key_block, preferred_element_type=jnp.float32
        )
        key_part = jnp.einsum(
            "kgqs,qkgd->skd", d_scores, query_groups, preferred_element_type=jnp.float32
        )
        value_part = jnp.einsum(
            "kgqs,qkgd->skd", probs_low, d_groups, preferred_element_type=jnp.float32
        )
        d_keys = lax.dynamic_update_slice_in_dim(
            d_keys, lax.dynamic_slice_in_dim(d_keys, start, block, 0) + key_part, start, 0
        )
        d_values = lax.dynamic_update_slice_in_dim(
            d_values, lax.dynamic_slice_in_dim(d_values, start, block, 0) + value_part, start, 0
        )
        return (d_query, d_keys, d_values)

    grad_init = (
        jnp.zeros((tokens, KV_HEADS, groups, HEAD_DIM), jnp.float32),
        jnp.zeros((length, KV_HEADS, HEAD_DIM), jnp.float32),
        jnp.zeros((length, KV_HEADS, HEAD_DIM), jnp.float32),
    )
    d_query, d_keys, d_values = lax.fori_loop(0, count, grad_step, grad_init)
    key_sum, value_sum = (
        lax.psum_scatter(
            (d_keys * scale).reshape(length, KV_HEADS * HEAD_DIM).astype(jnp.bfloat16),
            "dp",
            scatter_dimension=0,
            tiled=True,
        ).astype(jnp.float32),
        lax.psum_scatter(
            d_values.reshape(length, KV_HEADS * HEAD_DIM).astype(jnp.bfloat16),
            "dp",
            scatter_dimension=0,
            tiled=True,
        ).astype(jnp.float32),
    )
    d_query_low = (
        rotate_back((d_query * scale).reshape(tokens, HEADS, HEAD_DIM), cosine, sine)
        .astype(jnp.bfloat16)
        .reshape(tokens, HEADS * HEAD_DIM)
    )
    d_key_low = (
        rotate_back(key_sum.reshape(tokens, KV_HEADS, HEAD_DIM), cosine, sine)
        .astype(jnp.bfloat16)
        .reshape(tokens, KV_HEADS * HEAD_DIM)
    )
    d_value_low = value_sum.astype(jnp.bfloat16)
    grad_query_part = jnp.einsum(
        "td,tf->df", normed, d_query_low, preferred_element_type=jnp.float32
    )
    grad_key_part = jnp.einsum("td,tf->df", normed, d_key_low, preferred_element_type=jnp.float32)
    grad_value_part = jnp.einsum(
        "td,tf->df", normed, d_value_low, preferred_element_type=jnp.float32
    )
    d_normed = jnp.einsum("tf,df->td", d_query_low, w_query, preferred_element_type=jnp.float32)
    d_normed = d_normed + jnp.einsum(
        "tf,df->td", d_key_low, w_key, preferred_element_type=jnp.float32
    )
    d_normed = d_normed + jnp.einsum(
        "tf,df->td", d_value_low, w_value, preferred_element_type=jnp.float32
    )
    scaled_one = d_normed * gain_attn
    grad_gain_attn_part = jnp.sum(d_normed * inputs * inv_one, axis=0)
    grad_in = (
        d_middle
        + inv_one * scaled_one
        - inputs * inv_one**3 * jnp.mean(inputs * scaled_one, axis=-1, keepdims=True)
    )
    dense = (
        lax.psum_scatter(grad_gain_attn_part, ("dp", "expert"), scatter_dimension=0, tiled=True),
        lax.psum_scatter(grad_query_part, ("dp", "expert"), scatter_dimension=0, tiled=True),
        lax.psum_scatter(grad_key_part, ("dp", "expert"), scatter_dimension=0, tiled=True),
        lax.psum_scatter(grad_value_part, ("dp", "expert"), scatter_dimension=0, tiled=True),
        lax.psum_scatter(grad_output_part, ("dp", "expert"), scatter_dimension=0, tiled=True),
        lax.psum_scatter(grad_gain_mlp_part, ("dp", "expert"), scatter_dimension=0, tiled=True),
        lax.psum_scatter(grad_router_part, ("dp", "expert"), scatter_dimension=0, tiled=True),
    )
    return (
        hidden_out[None],
        grad_in[None],
        dense[0],
        dense[1],
        dense[2],
        dense[3],
        dense[4],
        dense[5],
        dense[6],
        gate_total,
        up_total,
        down_total,
    )


def solution(mesh):
    in_specs = (
        P("expert", "dp", None),
        P(),
        P(),
        P(),
        P(),
        P(),
        P(),
        P(),
        P("expert", None, None),
        P("expert", None, None),
        P("expert", None, None),
        P("expert", "dp", None),
        P("expert", "dp", None),
        P("expert", "dp", None),
    )
    out_specs = (
        P("expert", "dp", None),
        P("expert", "dp", None),
        P(("dp", "expert")),
        P(("dp", "expert"), None),
        P(("dp", "expert"), None),
        P(("dp", "expert"), None),
        P(("dp", "expert"), None),
        P(("dp", "expert")),
        P(("dp", "expert"), None),
        P("expert", "dp", None),
        P("expert", "dp", None),
        P("expert", "dp", None),
    )
    return jax.shard_map(body, mesh=mesh, in_specs=in_specs, out_specs=out_specs, check_vma=False)
```

profile of v0, /device:TPU:0, one launch (start us, length us, event | category | flops | bytes accessed | tf_op | source)
XLA Modules:
  0.0 2534.0 jit_solution(5355342469741384523)
XLA Ops:
  34.3 13.6 gather_fusion
  48.0 11.5 reduce-window.6
  60.5 13.6 gather_fusion.1
  124.9 70.6 %all-gather.3.cloned.1.call-done = bf16[2560,8,64]{2,1,0:T(8,128)(2,1)} async-done(((bf16[320,8,64]{2,1,0:T(8,128)(2,1)}), bf16[2560,8,64]{2,1,0:T(8,128)(2,1)}) %all-gather.3.cloned.1.call-update) | async-done | bytes 2621456 | tf_op jit(solution)/shard_map/all_gather | solution.py:109
  238.5 95.0 %all_to_all.20 = bf16[4,10,64,1536]{3,2,1,0:T(8,128)(2,1)} all-to-all(bf16[4,10,64,1536]{3,2,1,0:T(8,128)(2,1)} %broadcast_select_fusion.1), channel_id=1, replica_groups=mesh['dp'=8,'expert'=4] {'expert'}, dimensions={0} | all-to-all | bytes 15728640 | tf_op jit(solution)/shard_map/all_to_all | solution.py:172
  333.6 14.2 fusion.62
  347.8 16.7 fusion.86
  364.5 13.7 convert_bitcast_fusion
  393.1 85.8 %all-to-all-done.1 = bf16[4,10,64,1536]{3,2,1,0:T(8,128)(2,1)} async-done(((bf16[4,10,64,1536]{3,2,1,0:T(8,128)(2,1)}), bf16[4,10,64,1536]{3,2,1,0:T(8,128)(2,1)}, u32[]{:S(2)}, u32[]{:S(2)}) %all-to-all-start.1) | async-done | bytes 7864352 | tf_op jit(solution)/shard_map/all_to_all | solution.py:179
  485.8 20.9 gather_fusion.3
  526.1 20.6 gather_fusion.4
  553.7 95.3 %all_to_all.21 = bf16[4,10,64,1536]{3,2,1,0:T(8,128)(2,1)} all-to-all(bf16[4,10,64,1536]{3,2,1,0:T(8,128)(2,1)} %broadcast_select_fusion), channel_id=1, replica_groups=mesh['dp'=8,'expert'=4] {'expert'}, dimensions={0} | all-to-all | bytes 15728640 | tf_op jit(solution)/shard_map/all_to_all | solution.py:193
  649.0 15.8 fusion.84
  664.8 11.8 fusion.56
  676.7 15.9 fusion.69
  712.7 80.4 %all-to-all-done.3 = bf16[4,10,64,1536]{3,2,1,0:T(8,128)(2,1)} async-done(((bf16[4,10,64,1536]{3,2,1,0:T(8,128)(2,1)}), bf16[4,10,64,1536]{3,2,1,0:T(8,128)(2,1)}, u32[]{:S(2)}, u32[]{:S(2)}) %all-to-all-start.3) | async-done | bytes 7864352 | tf_op jit(solution)/shard_map/all_to_all | solution.py:224
  800.0 20.8 gather_fusion.5
  850.3 26.7 %while.41 = (s32[]{:T(128)}, f32[320,8,3,64]{0,3,2,1:T(8,128)}, f32[2560,8,64]{0,2,1:T(8,128)}, f32[2560,8,64]{0,2,1:T(8,128)}, s32[]{:T(128)}, /*index=5*/bf16[...) while((s32[]{:T(128)}, f32[320,8,3,64]{0,3,2,1:T(8,128)}, ...), condition=%wide.region_21.22_spmd.clone, body=%wide.region_20.21_spmd.clone.sunk | while | flops 2557084416 | bytes 89326328 | solution.py:295
  897.3 10.8 bitcast_convert_fusion
  908.2 10.7 bitcast_convert_fusion.2
  919.0 10.7 bitcast_convert_fusion.1
  929.8 167.0 %reduce-scatter.31.cloned.1.call-done = bf16[320,512]{1,0:T(8,128)(2,1)} async-done(((bf16[2560,512]{1,0:T(8,128)(2,1)}), bf16[320,512]{1,0:T(8,128)(2,1)}) %reduce-scatter.31.cloned.1.call-update) | async-done | bytes 327696
  1101.8 67.6 %reduce-scatter.33.cloned.1.call-done = bf16[320,512]{1,0:T(8,128)(2,1)} async-done(((bf16[2560,512]{1,0:T(8,128)(2,1)}), bf16[320,512]{1,0:T(8,128)(2,1)}) %reduce-scatter.33.cloned.1.call-update) | async-done | bytes 327696
  1190.4 78.4 %reduce-scatter.35.cloned.1.call-done = f32[48,40]{1,0:T(8,128)} async-done(((f32[1536,40]{1,0:T(8,128)}), f32[48,40]{1,0:T(8,128)}) %reduce-scatter.35.cloned.1.call-update) | async-done | bytes 7696
  1279.0 46.3 %all-reduce.4 = (f32[1536]{0:T(1024)}, f32[1536]{0:T(1024)}) all-reduce(f32[1536]{0:T(1024)} %get-tuple-element.315, f32[1536]{0:T(1024)} %get-tuple-element.313), channel_id=4, replica_groups=mesh['dp'=8,'expert'=4] {'dp','expert'}, use_global_device_ids=true, to_apply=%region_26.27.clone | all-reduce | flops 3072 | bytes 24576
  1332.4 191.1 %reduce-scatter.29.cloned.1.call-done = bf16[10,64,1536]{2,1,0:T(8,128)(2,1)} async-done(((bf16[10,512,1536]{2,1,0:T(8,128)(2,1)}), bf16[10,64,1536]{2,1,0:T(8,128)(2,1)}) %reduce-scatter.29.cloned.1.call-update) | async-done | bytes 1966096 | tf_op jit(solution)/shard_map/reduce_scatter | solution.py:216
  1527.5 249.8 %reduce-scatter.25.cloned.1.call-done = bf16[10,192,512]{2,1,0:T(8,128)(2,1)} async-done(((bf16[10,1536,512]{2,1,0:T(8,128)(2,1)}), bf16[10,192,512]{2,1,0:T(8,128)(2,1)}) %reduce-scatter.25.cloned.1.call-update) | async-done | bytes 1966096 | tf_op jit(solution)/shard_map/reduce_scatter | solution.py:210
  1781.3 249.8 %reduce-scatter.27.cloned.1.call-done = bf16[10,192,512]{2,1,0:T(8,128)(2,1)} async-done(((bf16[10,1536,512]{2,1,0:T(8,128)(2,1)}), bf16[10,192,512]{2,1,0:T(8,128)(2,1)}) %reduce-scatter.27.cloned.1.call-update) | async-done | bytes 1966096 | tf_op jit(solution)/shard_map/reduce_scatter | solution.py:213
  2035.1 102.6 %reduce-scatter.19.cloned.1.call-done = f32[48,512]{1,0:T(8,128)} async-done(((f32[1536,512]{1,0:T(8,128)}), f32[48,512]{1,0:T(8,128)}) %reduce-scatter.19.cloned.1.call-update) | async-done | bytes 98320 | tf_op jit(solution)/shard_map/reduce_scatter | solution.py:345
  2137.8 106.3 %reduce-scatter.21.cloned.1.call-done = f32[48,512]{1,0:T(8,128)} async-done(((f32[1536,512]{1,0:T(8,128)}), f32[48,512]{1,0:T(8,128)}) %reduce-scatter.21.cloned.1.call-update) | async-done | bytes 98320 | tf_op jit(solution)/shard_map/reduce_scatter | solution.py:346
  2244.1 140.9 %reduce-scatter.23.cloned.1.call-done = f32[48,1536]{1,0:T(8,128)} async-done(((f32[1536,1536]{1,0:T(8,128)}), f32[48,1536]{1,0:T(8,128)}) %reduce-scatter.23.cloned.1.call-update) | async-done | bytes 294928 | tf_op jit(solution)/shard_map/reduce_scatter | solution.py:347
  2385.0 141.9 %reduce-scatter.17.cloned.1.call-done = f32[48,1536]{1,0:T(8,128)} async-done(((f32[1536,1536]{1,0:T(8,128)}), f32[48,1536]{1,0:T(8,128)}) %reduce-scatter.17.cloned.1.call-update) | async-done | bytes 294928 | tf_op jit(solution)/shard_map/reduce_scatter | solution.py:344
  (289 shorter events, 346.6 us)
Async XLA Ops:
  7.2 12.0 copy-start
  7.2 101.0 %all-gather.5.cloned.1.call-start = ((), (), s32[]{:S(2)}) async-start(), calls=%async_computation.15 | async-start | bytes 5898240 | tf_op jit(solution)/shard_map/all_gather | solution.py:108
  19.1 176.5 %all-gather.3.cloned.1.call-start = ((), (), s32[]{:S(2)}) async-start(), calls=%async_computation.14 | async-start | bytes 5898240 | tf_op jit(solution)/shard_map/all_gather | solution.py:109
  84.8 146.8 %copy-start.45 = (pred[4,10,64]{2,1,0:T(8,128)(4,1)}, pred[4,10,64]{2,1,0:T(8,128)(4,1)S(1)}, u32[]{:S(2)}) copy-start(pred[4,10,64]{2,1,0:T(8,128)(4,1)S(1)} %broadcast_in_dim.67) | copy-start | bytes 7684
  221.1 10.5 copy-start.55
  222.0 170.0 %copy-start.1 = (bf16[320,1536]{1,0:T(8,128)(2,1)}, bf16[320,1536]{1,0:T(8,128)(2,1)S(1)}, u32[]{:S(2)}) copy-start(bf16[320,1536]{1,0:T(8,128)(2,1)S(1)} %multiply_convert_fusion.1) | copy-start | bytes 2949124
  385.4 93.5 %all-to-all-start.1 = ((bf16[4,10,64,1536]{3,2,1,0:T(8,128)(2,1)}), bf16[4,10,64,1536]{3,2,1,0:T(8,128)(2,1)}, u32[]{:S(2)}, u32[]{:S(2)}) async-start(bf16[4,10,64,1536]{3,2,1,0:T(8,128)(2,1)} %copy.90), calls=%async_computation.1 | async-start | bytes 15728640 | tf_op jit(solution)/shard_map/all_to_all | solution.py:179
  485.8 20.9 copy-start.16
  526.1 20.6 copy-start.46
  699.9 93.2 %all-to-all-start.3 = ((bf16[4,10,64,1536]{3,2,1,0:T(8,128)(2,1)}), bf16[4,10,64,1536]{3,2,1,0:T(8,128)(2,1)}, u32[]{:S(2)}, u32[]{:S(2)}) async-start(bf16[4,10,64,1536]{3,2,1,0:T(8,128)(2,1)} %copy.93), calls=%async_computation.3 | async-start | bytes 15728640 | tf_op jit(solution)/shard_map/all_to_all | solution.py:224
  705.6 391.2 %reduce-scatter.31.cloned.1.call-start = ((), (), s32[]{:S(2)}) async-start(), calls=%async_computation.23 | async-start | bytes 2949120
  820.8 8.7 copy-start.9
  820.8 8.7 copy-start.34
  820.8 8.7 copy-start.35
  820.8 8.7 copy-start.48
  820.8 8.7 copy-start.56
  885.9 283.5 %reduce-scatter.33.cloned.1.call-start = ((), (), s32[]{:S(2)}) async-start(), calls=%async_computation.24 | async-start | bytes 2949120
  894.7 374.1 %reduce-scatter.35.cloned.1.call-start = ((), (), s32[]{:S(2)}) async-start(), calls=%async_computation.25 | async-start | bytes 811008
  897.3 626.3 %reduce-scatter.29.cloned.1.call-start = ((), (), s32[]{:S(2)}) async-start(), calls=%async_computation.22 | async-start | bytes 17694720 | tf_op jit(solution)/shard_map/reduce_scatter | solution.py:216
  908.2 869.1 %reduce-scatter.25.cloned.1.call-start = ((), (), s32[]{:S(2)}) async-start(), calls=%async_computation.20 | async-start | bytes 17694720 | tf_op jit(solution)/shard_map/reduce_scatter | solution.py:210
  918.9 1112.2 %reduce-scatter.27.cloned.1.call-start = ((), (), s32[]{:S(2)}) async-start(), calls=%async_computation.21 | async-start | bytes 17694720 | tf_op jit(solution)/shard_map/reduce_scatter | solution.py:213
  929.7 168.4 %copy-start.27 = (f32[320,32]{0,1:T(8,128)S(1)}, f32[320,32]{0,1:T(8,128)}, u32[]{:S(2)}) copy-start(f32[320,32]{0,1:T(8,128)} %copy-done.25) | copy-start | bytes 122884
  929.7 168.4 %copy-start.31 = (f32[320,32]{0,1:T(8,128)S(1)}, f32[320,32]{0,1:T(8,128)}, u32[]{:S(2)}) copy-start(f32[320,32]{0,1:T(8,128)} %copy-done.29) | copy-start | bytes 122884
  929.7 169.3 %copy-start.14 = (bf16[1,320,1536]{2,1,0:T(8,128)(2,1)S(1)}, bf16[1,320,1536]{2,1,0:T(8,128)(2,1)}, u32[]{:S(2)}) copy-start(bf16[1,320,1536]{2,1,0:T(8,128)(2,1)} %copy-done.12) | copy-start | bytes 2949124
  929.7 1208.1 %reduce-scatter.19.cloned.1.call-start = ((), (), s32[]{:S(2)}) async-start(), calls=%async_computation.17 | async-start | bytes 3244032 | tf_op jit(solution)/shard_map/reduce_scatter | solution.py:345
  1101.7 67.7 %copy-start.7 = (f32[1,320,1536]{2,1,0:T(8,128)S(1)}, f32[1,320,1536]{2,1,0:T(8,128)}, u32[]{:S(2)}) copy-start(f32[1,320,1536]{2,1,0:T(8,128)} %param.20) | copy-start | bytes 5898244
  1101.7 67.7 %copy-start.42 = (f32[1536]{0:T(1024)S(1)}, f32[1536]{0:T(1024)}, u32[]{:S(2)}) copy-start(f32[1536]{0:T(1024)} %param.21) | copy-start | bytes 18436
  1101.7 67.7 %copy-start.50 = (f32[320]{0:T(512)S(1)}, f32[320]{0:T(512)}, u32[]{:S(2)}) copy-start(f32[320]{0:T(512)} %copy-done.49) | copy-start | bytes 3844
  1101.7 1142.4 %reduce-scatter.21.cloned.1.call-start = ((), (), s32[]{:S(2)}) async-start(), calls=%async_computation.18 | async-start | bytes 3244032 | tf_op jit(solution)/shard_map/reduce_scatter | solution.py:346
  1173.3 1211.8 %reduce-scatter.23.cloned.1.call-start = ((), (), s32[]{:S(2)}) async-start(), calls=%async_computation.19 | async-start | bytes 9732096 | tf_op jit(solution)/shard_map/reduce_scatter | solution.py:347
  1181.6 1345.4 %reduce-scatter.17.cloned.1.call-start = ((), (), s32[]{:S(2)}) async-start(), calls=%async_computation.16 | async-start | bytes 9732096 | tf_op jit(solution)/shard_map/reduce_scatter | solution.py:344
  1276.2 52.2 %copy-start.58 = (f32[320]{0:T(512)S(1)}, f32[320]{0:T(512)}, u32[]{:S(2)}) copy-start(f32[320]{0:T(512)} %get-tuple-element.395) | copy-start | bytes 3844
  (46 other events, 186.6 us)
Sparse Core Ops, SparseCore 0:
  19.2 88.9 all-gather.4
  110.9 84.5 all-gather.2
  886.0 210.6 reduce-scatter.30
  1100.2 69.2 reduce-scatter.32
  1174.4 94.3 reduce-scatter.34
  1272.2 251.2 reduce-scatter.28
  1527.1 250.1 reduce-scatter.24
  1780.9 250.2 reduce-scatter.26
  2037.1 100.5 reduce-scatter.18
  2143.6 100.4 reduce-scatter.20
  2250.6 134.4 reduce-scatter.22
  2392.4 134.5 reduce-scatter.16
where the time goes:
time: 2540 us; the launch traced here: 2530 us
  waiting for transfers between devices  1740 us (69%)
  blocking collectives  237 us (9%)
  matrix products  220 us (9%)
  local copies, waits for them, and re-layouts  212 us (8%)
  other arithmetic  95.4 us (4%)
    unnamed x15, waiting for transfers between devices  313 us
    reduce_scatter x1, waiting for transfers between devices, body(): lax.psum_scatter(grad_up_part.astype(jnp.bfloat16), 'dp', scatter_dimensi...  250 us
    reduce_scatter x1, waiting for transfers between devices, body(): lax.psum_scatter(grad_gate_part.astype(jnp.bfloat16), 'dp', scatter_dimen...  250 us
    reduce_scatter x1, waiting for transfers between devices, body(): lax.psum_scatter(grad_down_part.astype(jnp.bfloat16), 'dp', scatter_dimen...  191 us
    reduce_scatter x1, waiting for transfers between devices, body(): lax.psum_scatter(grad_query_part, ('dp', 'expert'), scatter_dimension=0,...  142 us
    reduce_scatter x1, waiting for transfers between devices, body(): lax.psum_scatter(grad_output_part, ('dp', 'expert'), scatter_dimension=0,...  141 us
    reduce_scatter x1, waiting for transfers between devices, body(): lax.psum_scatter(grad_value_part, ('dp', 'expert'), scatter_dimension=0,...  106 us
    reduce_scatter x1, waiting for transfers between devices, body(): lax.psum_scatter(grad_key_part, ('dp', 'expert'), scatter_dimension=0, ti...  103 us
  transfers between devices with their start and end apart: 14, of which 14 were waited for; matrix products, arithmetic and copies ran while one was open for 8% of the time, Pallas kernels for 0%

commit v1 on v0

--- a/solution.py
+++ b/solution.py
@@ -9,6 +9,11 @@
 HEAD_DIM = 64
 EPS = 1e-05
 MASKED = -1e30
+
+
+def swapped_in(array, axis, dim):
+    repeated = jnp.stack([array] * lax.axis_size(axis))
+    return jnp.concatenate(lax.all_to_all(repeated, axis, 0, 0), axis=dim)
 
 
 def rotary_tables(positions):
@@ -106,7 +111,7 @@
     )
     keys_all, values_all = (
         lax.all_gather(keys_low, "dp", axis=0, tiled=True),
-        lax.all_gather(values_low, "dp", axis=0, tiled=True),
+        swapped_in(values_low, "dp", 0),
     )
     query_groups = queries.reshape(tokens, KV_HEADS, groups, HEAD_DIM)
 

time: 2540 us -> 2570 us (1.012)
    all_gather x1, waiting for transfers between devices: 70.6 us -> 163 us  [body(): lax.all_gather(values_low, 'dp', axis=0, tiled=True)]
    all_to_all x1, waiting for transfers between devices: 80.4 us -> 0.01 us  [body(): lax.all_to_all(d_rows, 'expert', split_axis=0, concat_axis=0, tiled=True)]
    unnamed x15, waiting for transfers between devices: 313 us -> 276 us
    all_to_all x0 -> x1, waiting for transfers between devices: none -> 27.2 us  [swapped_in(): return jnp.concatenate(lax.all_to_all(repeated, axis, 0, 0), axis=dim)]
  transfers between devices with their start and end apart: 14 -> 15, of which waited for: 14 -> 14; matrix products, arithmetic and copies ran while one was open for 8% -> 8% of each run, Pallas kernels for 0% -> 0%
where the time goes in v1:
time: 2570 us; the launch traced here: 2560 us
  waiting for transfers between devices  1750 us (68%)
  blocking collectives  237 us (9%)
  local copies, waits for them, and re-layouts  226 us (9%)
  matrix products  221 us (9%)
  other arithmetic  93.4 us (4%)
    unnamed x15, waiting for transfers between devices  276 us
    reduce_scatter x1, waiting for transfers between devices, body(): lax.psum_scatter(grad_up_part.astype(jnp.bfloat16), 'dp', scatter_dimensi...  250 us
    reduce_scatter x1, waiting for transfers between devices, body(): lax.psum_scatter(grad_gate_part.astype(jnp.bfloat16), 'dp', scatter_dimen...  250 us
    reduce_scatter x1, waiting for transfers between devices, body(): lax.psum_scatter(grad_down_part.astype(jnp.bfloat16), 'dp', scatter_dimen...  191 us
    all_gather x1, waiting for transfers between devices, body(): lax.all_gather(values_low, 'dp', axis=0, tiled=True)  163 us
    reduce_scatter x1, waiting for transfers between devices, body(): lax.psum_scatter(grad_query_part, ('dp', 'expert'), scatter_dimension=0,...  142 us
    reduce_scatter x1, waiting for transfers between devices, body(): lax.psum_scatter(grad_output_part, ('dp', 'expert'), scatter_dimension=0,...  141 us
    reduce_scatter x1, waiting for transfers between devices, body(): lax.psum_scatter(grad_value_part, ('dp', 'expert'), scatter_dimension=0,...  106 us
  transfers between devices with their start and end apart: 15, of which 14 were waited for; matrix products, arithmetic and copies ran while one was open for 8% of the time, Pallas kernels for 0%

profile of v1, /device:TPU:0, one launch (start us, length us, event | category | flops | bytes accessed | tf_op | source)
XLA Modules:
  0.0 2559.8 jit_solution(6523308436356698055)
XLA Ops:
  41.9 13.6 gather_fusion
  56.2 11.5 reduce-window.6
  70.7 13.6 gather_fusion.1
  107.7 27.2 %all-to-all-done = bf16[8,320,8,64]{1,3,2,0:T(8,128)(2,1)} async-done(((bf16[8,320,8,64]{1,3,2,0:T(8,128)(2,1)}), bf16[8,320,8,64]{1,3,2,0:T(8,128)(2,1)}, u32[]{:S(2)}, u32[]{:S(2)}) %all-to-all-start) | async-done | bytes 2621472 | tf_op jit(solution)/shard_map/all_to_all | solution.py:16
  146.2 11.2 all-gather.3.cloned.1.call-done
  210.3 95.0 %all_to_all.25 = bf16[4,10,64,1536]{3,2,1,0:T(8,128)(2,1)} all-to-all(bf16[4,10,64,1536]{3,2,1,0:T(8,128)(2,1)} %broadcast_select_fusion.1), channel_id=1, replica_groups=mesh['dp'=8,'expert'=4] {'expert'}, dimensions={0} | all-to-all | bytes 15728640 | tf_op jit(solution)/shard_map/all_to_all | solution.py:177
  305.3 14.2 fusion.62
  319.5 16.7 fusion.86
  336.2 13.7 convert_bitcast_fusion
  364.8 85.8 %all-to-all-done.2 = bf16[4,10,64,1536]{3,2,1,0:T(8,128)(2,1)} async-done(((bf16[4,10,64,1536]{3,2,1,0:T(8,128)(2,1)}), bf16[4,10,64,1536]{3,2,1,0:T(8,128)(2,1)}, u32[]{:S(2)}, u32[]{:S(2)}) %all-to-all-start.2) | async-done | bytes 7864352 | tf_op jit(solution)/shard_map/all_to_all | solution.py:184
  457.4 20.9 gather_fusion.3
  497.7 20.6 gather_fusion.4
  525.4 95.3 %all_to_all.26 = bf16[4,10,64,1536]{3,2,1,0:T(8,128)(2,1)} all-to-all(bf16[4,10,64,1536]{3,2,1,0:T(8,128)(2,1)} %broadcast_select_fusion), channel_id=1, replica_groups=mesh['dp'=8,'expert'=4] {'expert'}, dimensions={0} | all-to-all | bytes 15728640 | tf_op jit(solution)/shard_map/all_to_all | solution.py:198
  620.6 15.8 fusion.84
  636.5 11.9 fusion.56
  648.4 15.9 fusion.69
  678.6 163.4 %all-gather.5.cloned.1.call-done = bf16[2560,8,64]{2,1,0:T(8,128)(2,1)} async-done(((bf16[320,8,64]{2,1,0:T(8,128)(2,1)}), bf16[2560,8,64]{2,1,0:T(8,128)(2,1)}) %all-gather.5.cloned.1.call-update) | async-done | bytes 2621456 | tf_op jit(solution)/shard_map/all_gather | solution.py:263
  862.7 20.8 gather_fusion.5
  912.9 26.6 %while.41 = (s32[]{:T(128)}, f32[320,8,3,64]{0,3,2,1:T(8,128)}, f32[2560,8,64]{0,2,1:T(8,128)}, f32[2560,8,64]{0,2,1:T(8,128)}, s32[]{:T(128)}, /*index=5*/bf16[...) while((s32[]{:T(128)}, f32[320,8,3,64]{0,3,2,1:T(8,128)}, ...), condition=%wide.region_21.22_spmd.clone, body=%wide.region_20.21_spmd.clone.sunk | while | flops 2557084416 | bytes 89326328 | solution.py:300
  959.9 10.7 bitcast_convert_fusion
  981.4 10.6 bitcast_convert_fusion.1
  992.2 129.8 %reduce-scatter.31.cloned.1.call-done = bf16[320,512]{1,0:T(8,128)(2,1)} async-done(((bf16[2560,512]{1,0:T(8,128)(2,1)}), bf16[320,512]{1,0:T(8,128)(2,1)}) %reduce-scatter.31.cloned.1.call-update) | async-done | bytes 327696
  1127.0 67.8 %reduce-scatter.33.cloned.1.call-done = bf16[320,512]{1,0:T(8,128)(2,1)} async-done(((bf16[2560,512]{1,0:T(8,128)(2,1)}), bf16[320,512]{1,0:T(8,128)(2,1)}) %reduce-scatter.33.cloned.1.call-update) | async-done | bytes 327696
  1215.7 78.4 %reduce-scatter.35.cloned.1.call-done = f32[48,40]{1,0:T(8,128)} async-done(((f32[1536,40]{1,0:T(8,128)}), f32[48,40]{1,0:T(8,128)}) %reduce-scatter.35.cloned.1.call-update) | async-done | bytes 7696
  1304.3 46.3 %all-reduce.4 = (f32[1536]{0:T(1024)}, f32[1536]{0:T(1024)}) all-reduce(f32[1536]{0:T(1024)} %get-tuple-element.342, f32[1536]{0:T(1024)} %get-tuple-element.340), channel_id=4, replica_groups=mesh['dp'=8,'expert'=4] {'dp','expert'}, use_global_device_ids=true, to_apply=%region_26.27.clone | all-reduce | flops 3072 | bytes 24576
  1357.8 191.1 %reduce-scatter.29.cloned.1.call-done = bf16[10,64,1536]{2,1,0:T(8,128)(2,1)} async-done(((bf16[10,512,1536]{2,1,0:T(8,128)(2,1)}), bf16[10,64,1536]{2,1,0:T(8,128)(2,1)}) %reduce-scatter.29.cloned.1.call-update) | async-done | bytes 1966096 | tf_op jit(solution)/shard_map/reduce_scatter | solution.py:221
  1552.8 249.9 %reduce-scatter.25.cloned.1.call-done = bf16[10,192,512]{2,1,0:T(8,128)(2,1)} async-done(((bf16[10,1536,512]{2,1,0:T(8,128)(2,1)}), bf16[10,192,512]{2,1,0:T(8,128)(2,1)}) %reduce-scatter.25.cloned.1.call-update) | async-done | bytes 1966096 | tf_op jit(solution)/shard_map/reduce_scatter | solution.py:215
  1806.7 249.9 %reduce-scatter.27.cloned.1.call-done = bf16[10,192,512]{2,1,0:T(8,128)(2,1)} async-done(((bf16[10,1536,512]{2,1,0:T(8,128)(2,1)}), bf16[10,192,512]{2,1,0:T(8,128)(2,1)}) %reduce-scatter.27.cloned.1.call-update) | async-done | bytes 1966096 | tf_op jit(solution)/shard_map/reduce_scatter | solution.py:218
  2060.6 102.6 %reduce-scatter.19.cloned.1.call-done = f32[48,512]{1,0:T(8,128)} async-done(((f32[1536,512]{1,0:T(8,128)}), f32[48,512]{1,0:T(8,128)}) %reduce-scatter.19.cloned.1.call-update) | async-done | bytes 98320 | tf_op jit(solution)/shard_map/reduce_scatter | solution.py:350
  2163.2 106.4 %reduce-scatter.21.cloned.1.call-done = f32[48,512]{1,0:T(8,128)} async-done(((f32[1536,512]{1,0:T(8,128)}), f32[48,512]{1,0:T(8,128)}) %reduce-scatter.21.cloned.1.call-update) | async-done | bytes 98320 | tf_op jit(solution)/shard_map/reduce_scatter | solution.py:351
  2269.6 141.1 %reduce-scatter.23.cloned.1.call-done = f32[48,1536]{1,0:T(8,128)} async-done(((f32[1536,1536]{1,0:T(8,128)}), f32[48,1536]{1,0:T(8,128)}) %reduce-scatter.23.cloned.1.call-update) | async-done | bytes 294928 | tf_op jit(solution)/shard_map/reduce_scatter | solution.py:352
  2410.7 142.0 %reduce-scatter.17.cloned.1.call-done = f32[48,1536]{1,0:T(8,128)} async-done(((f32[1536,1536]{1,0:T(8,128)}), f32[48,1536]{1,0:T(8,128)}) %reduce-scatter.17.cloned.1.call-update) | async-done | bytes 294928 | tf_op jit(solution)/shard_map/reduce_scatter | solution.py:349
  (300 shorter events, 369.1 us)
Async XLA Ops:
  15.1 119.8 %all-to-all-start = ((bf16[8,320,8,64]{1,3,2,0:T(8,128)(2,1)}), bf16[8,320,8,64]{1,3,2,0:T(8,128)(2,1)}, u32[]{:S(2)}, u32[]{:S(2)}) async-start(bf16[8,320,8,64]{1,3,2,0:T(8,128)(2,1)} %stack.3), calls=%async_computation | async-start | bytes 6291456 | tf_op jit(solution)/shard_map/all_to_all | solution.py:16
  22.5 134.9 %all-gather.3.cloned.1.call-start = ((), (), s32[]{:S(2)}) async-start(), calls=%async_computation.15 | async-start | bytes 5898240 | tf_op jit(solution)/shard_map/all_gather | solution.py:113
  31.9 23.6 copy-start.54
  70.7 13.6 copy-start.58
  95.4 108.0 %copy-start.46 = (pred[4,10,64]{2,1,0:T(8,128)(4,1)}, pred[4,10,64]{2,1,0:T(8,128)(4,1)S(1)}, u32[]{:S(2)}) copy-start(pred[4,10,64]{2,1,0:T(8,128)(4,1)S(1)} %broadcast_in_dim.67) | copy-start | bytes 7684
  193.7 169.9 %copy-start.1 = (bf16[320,1536]{1,0:T(8,128)(2,1)}, bf16[320,1536]{1,0:T(8,128)(2,1)S(1)}, u32[]{:S(2)}) copy-start(bf16[320,1536]{1,0:T(8,128)(2,1)S(1)} %multiply_convert_fusion.1) | copy-start | bytes 2949124
  357.1 93.5 %all-to-all-start.2 = ((bf16[4,10,64,1536]{3,2,1,0:T(8,128)(2,1)}), bf16[4,10,64,1536]{3,2,1,0:T(8,128)(2,1)}, u32[]{:S(2)}, u32[]{:S(2)}) async-start(bf16[4,10,64,1536]{3,2,1,0:T(8,128)(2,1)} %copy.114), calls=%async_computation.2 | async-start | bytes 15728640 | tf_op jit(solution)/shard_map/all_to_all | solution.py:184
  457.4 20.9 copy-start.15
  497.7 20.6 copy-start.47
  671.5 184.3 %all-to-all-start.4 = ((bf16[4,10,64,1536]{3,2,1,0:T(8,128)(2,1)}), bf16[4,10,64,1536]{3,2,1,0:T(8,128)(2,1)}, u32[]{:S(2)}, u32[]{:S(2)}) async-start(bf16[4,10,64,1536]{3,2,1,0:T(8,128)(2,1)} %copy.117), calls=%async_computation.4 | async-start | bytes 15728640 | tf_op jit(solution)/shard_map/all_to_all | solution.py:229
  677.2 164.8 %all-gather.5.cloned.1.call-start = ((), (), s32[]{:S(2)}) async-start(), calls=%async_computation.16 | async-start | bytes 5898240 | tf_op jit(solution)/shard_map/all_gather | solution.py:263
  678.5 443.5 %reduce-scatter.31.cloned.1.call-start = ((), (), s32[]{:S(2)}) async-start(), calls=%async_computation.24 | async-start | bytes 2949120
  678.5 170.3 %copy-start.40 = (f32[320,8]{0,1:T(8,128)S(1)}, f32[320,8]{0,1:T(8,128)}, u32[]{:S(2)}) copy-start(f32[320,8]{0,1:T(8,128)} %get-tuple-element.403) | copy-start | bytes 30724
  678.5 171.1 %copy-start.44 = (f32[320,1,8]{0,2,1:T(8,128)S(1)}, f32[320,1,8]{0,2,1:T(8,128)}, u32[]{:S(2)}) copy-start(f32[320,1,8]{0,2,1:T(8,128)} %copy.138) | copy-start | bytes 30724
  678.6 171.1 %copy-start.63 = (f32[320]{0:T(512)S(1)}, f32[320]{0:T(512)}, u32[]{:S(2)}) copy-start(f32[320]{0:T(512)} %get-tuple-element.402) | copy-start | bytes 3844
  678.6 171.1 %copy-start.39 = (s32[1,320,8]{1,2,0:T(8,128)S(1)}, s32[1,320,8]{1,2,0:T(8,128)}, u32[]{:S(2)}) copy-start(s32[1,320,8]{1,2,0:T(8,128)} %param.31) | copy-start | bytes 30724
  948.5 246.2 %reduce-scatter.33.cloned.1.call-start = ((), (), s32[]{:S(2)}) async-start(), calls=%async_computation.25 | async-start | bytes 2949120
  957.3 336.9 %reduce-scatter.35.cloned.1.call-start = ((), (), s32[]{:S(2)}) async-start(), calls=%async_computation.26 | async-start | bytes 811008
  959.9 589.0 %reduce-scatter.29.cloned.1.call-start = ((), (), s32[]{:S(2)}) async-start(), calls=%async_computation.23 | async-start | bytes 17694720 | tf_op jit(solution)/shard_map/reduce_scatter | solution.py:221
  970.7 832.0 %reduce-scatter.25.cloned.1.call-start = ((), (), s32[]{:S(2)}) async-start(), calls=%async_computation.21 | async-start | bytes 17694720 | tf_op jit(solution)/shard_map/reduce_scatter | solution.py:215
  981.4 1075.2 %reduce-scatter.27.cloned.1.call-start = ((), (), s32[]{:S(2)}) async-start(), calls=%async_computation.22 | async-start | bytes 17694720 | tf_op jit(solution)/shard_map/reduce_scatter | solution.py:218
  992.1 131.1 %copy-start.27 = (f32[320,32]{0,1:T(8,128)S(1)}, f32[320,32]{0,1:T(8,128)}, u32[]{:S(2)}) copy-start(f32[320,32]{0,1:T(8,128)} %copy-done.25) | copy-start | bytes 122884
  992.1 131.1 %copy-start.31 = (f32[320,32]{0,1:T(8,128)S(1)}, f32[320,32]{0,1:T(8,128)}, u32[]{:S(2)}) copy-start(f32[320,32]{0,1:T(8,128)} %copy-done.29) | copy-start | bytes 122884
  992.1 132.0 %copy-start.13 = (bf16[1,320,1536]{2,1,0:T(8,128)(2,1)S(1)}, bf16[1,320,1536]{2,1,0:T(8,128)(2,1)}, u32[]{:S(2)}) copy-start(bf16[1,320,1536]{2,1,0:T(8,128)(2,1)} %multiply_convert_fusion.2) | copy-start | bytes 2949124
  992.1 1171.1 %reduce-scatter.19.cloned.1.call-start = ((), (), s32[]{:S(2)}) async-start(), calls=%async_computation.18 | async-start | bytes 3244032 | tf_op jit(solution)/shard_map/reduce_scatter | solution.py:350
  1126.9 67.8 %copy-start.7 = (f32[1,320,1536]{2,1,0:T(8,128)S(1)}, f32[1,320,1536]{2,1,0:T(8,128)}, u32[]{:S(2)}) copy-start(f32[1,320,1536]{2,1,0:T(8,128)} %param.20) | copy-start | bytes 5898244
  1126.9 67.8 %copy-start.42 = (f32[1536]{0:T(1024)S(1)}, f32[1536]{0:T(1024)}, u32[]{:S(2)}) copy-start(f32[1536]{0:T(1024)} %param.21) | copy-start | bytes 18436
  1126.9 67.8 %copy-start.51 = (f32[320]{0:T(512)S(1)}, f32[320]{0:T(512)}, u32[]{:S(2)}) copy-start(f32[320]{0:T(512)} %copy-done.50) | copy-start | bytes 3844
  1126.9 1142.7 %reduce-scatter.21.cloned.1.call-start = ((), (), s32[]{:S(2)}) async-start(), calls=%async_computation.19 | async-start | bytes 3244032 | tf_op jit(solution)/shard_map/reduce_scatter | solution.py:351
  1198.6 1212.2 %reduce-scatter.23.cloned.1.call-start = ((), (), s32[]{:S(2)}) async-start(), calls=%async_computation.20 | async-start | bytes 9732096 | tf_op jit(solution)/shard_map/reduce_scatter | solution.py:352
  1206.9 1345.8 %reduce-scatter.17.cloned.1.call-start = ((), (), s32[]{:S(2)}) async-start(), calls=%async_computation.17 | async-start | bytes 9732096 | tf_op jit(solution)/shard_map/reduce_scatter | solution.py:349
  1301.6 52.3 %copy-start.62 = (f32[320]{0:T(512)S(1)}, f32[320]{0:T(512)}, u32[]{:S(2)}) copy-start(f32[320]{0:T(512)} %get-tuple-element.422) | copy-start | bytes 3844
  (50 other events, 233.1 us)
Sparse Core Ops, SparseCore 0:
  30.9 126.4 all-gather.2
  680.8 161.1 all-gather.4
  948.6 173.3 reduce-scatter.30
  1125.3 69.3 reduce-scatter.32
  1199.7 94.4 reduce-scatter.34
  1297.6 251.2 reduce-scatter.28
  1552.4 250.2 reduce-scatter.24
  1806.3 250.2 reduce-scatter.26
  2062.6 100.5 reduce-scatter.18
  2169.1 100.4 reduce-scatter.20
  2276.1 134.5 reduce-scatter.22
  2418.1 134.6 reduce-scatter.16
